TPU v7x, 512 devices: a whole 4x4x16 slice. The times are simulated.
512 devices in a mesh: dp: 64 (over x, z), tensor: 8 (over y, core).
Axes of the slice: x: 4, y: 4, z: 16, core: 2. Of those that a mesh axis runs over, the one named last changes fastest.
Arguments:
- tokens: bfloat16 [8192, 8192], P('dp', 'tensor'), may hold values from -6 to 6
- hidden_grad: bfloat16 [8192, 28672], P('dp', 'tensor'), may hold values from -0.0625 to 0.0625
- masters: float32 [8, 64, 128, 128], P('tensor', 'dp'), may hold values from -0.5 to 0.5
- block_row: int32 [8, 32], P('tensor'), may hold values from 0 to 63, as said below
- block_col: int32 [8, 32], P('tensor'), may hold values from 0 to 27
- owners: int32 [8, 64], P('tensor'), may hold values from 0 to 63, as said below
Outputs:
- grads: float32 [8, 192, 128, 128], P('tensor', 'dp')
Inputs may be any that keep to these rules, and one draw needn't show every extreme that they name: `block_row`: in each slice the kept places are distinct. `owners`: in each slice every owner takes at most 3 of the 64 kept blocks, and some owner takes exactly 3.
All inputs are finite; a program needn't handle non-finite values.
Results may differ from a plain program's by a relative error of at most 0.0044.
Values may be sent and summed in bfloat16 or wider, within the bound.
A program may use at most 64 MiB of HBM per device.

v0:
```python
import jax
import jax.numpy as jnp
from jax import lax
from jax.sharding import PartitionSpec as P


def slot_index(owner_row, capacity):
    count_all = owner_row.shape[0]
    same_owner = owner_row[:, None] == owner_row[None, :]
    earlier = (
        jnp.arange(count_all, dtype=jnp.int32)[None, :]
        < jnp.arange(count_all, dtype=jnp.int32)[:, None]
    )
    rank_index = jnp.sum(
        jnp.logical_and(same_owner, earlier).astype(jnp.int32), axis=1, dtype=jnp.int32
    )
    return owner_row * capacity + rank_index


def column_total(part, same_column):
    return jnp.einsum("tjc,kj->tkc", part, same_column, precision=lax.Precision.HIGHEST)


def local(tokens, hidden_grad, masters, block_row, block_col, owners):
    high = lax.Precision.HIGHEST
    features = lax.all_gather(tokens, "tensor", axis=1, tiled=True)
    token_count = features.shape[0]
    block_side = masters.shape[-1]
    kept_count = block_row.shape[1]
    weights = lax.all_gather(masters.astype(jnp.bfloat16), "dp", axis=1, tiled=True)[0]
    row_index = block_row[0]
    column_index = block_col[0]
    by_block = features.reshape(token_count, features.shape[1] // block_side, block_side)
    selected = jnp.take(by_block, row_index, axis=1)
    gate_part = jnp.einsum(
        "tkb,kbc->tkc", selected, weights[:kept_count], preferred_element_type=jnp.float32
    )
    up_part = jnp.einsum(
        "tkb,kbc->tkc", selected, weights[kept_count:], preferred_element_type=jnp.float32
    )
    same_column = (column_index[:, None] == column_index[None, :]).astype(jnp.float32)
    gate_value = column_total(gate_part, same_column)
    up_value = column_total(up_part, same_column)
    grad_columns = hidden_grad.reshape(token_count, hidden_grad.shape[1] // block_side, block_side)
    upstream = jnp.take(grad_columns, column_index, axis=1).astype(jnp.float32)
    sigmoid_gate = jax.nn.sigmoid(gate_value)
    gate_grad = (
        upstream * up_value * sigmoid_gate * (1.0 + gate_value * (1.0 - sigmoid_gate))
    ).astype(jnp.bfloat16)
    up_grad = (upstream * gate_value * sigmoid_gate).astype(jnp.bfloat16)
    grad_gate = jnp.einsum("tkb,tkc->kbc", selected, gate_grad, preferred_element_type=jnp.float32)
    grad_up = jnp.einsum("tkb,tkc->kbc", selected, up_grad, preferred_element_type=jnp.float32)
    block_grads = jnp.concatenate([grad_gate, grad_up], axis=0)
    owner_count = lax.axis_size("dp")
    capacity = 3 * block_grads.shape[0] // owner_count
    slot_list = slot_index(owners[0], capacity)
    summed = lax.psum(block_grads, "dp")
    own_slots = lax.axis_index("dp") * capacity + jnp.arange(capacity, dtype=jnp.int32)
    selector = (own_slots[:, None] == slot_list[None, :]).astype(jnp.float32)
    result = jnp.einsum("sk,kbc->sbc", selector, summed, precision=high)
    return result[None]


def solution(mesh):
    return jax.shard_map(
        local,
        mesh=mesh,
        in_specs=(
            P("dp", "tensor"),
            P("dp", "tensor"),
            P("tensor", "dp", None, None),
            P("tensor", None),
            P("tensor", None),
            P("tensor", None),
        ),
        out_specs=P("tensor", "dp", None, None),
        check_vma=False,
    )
```

profile of v0, /device:TPU:8, one launch (start us, length us, event | category | flops | bytes accessed | tf_op | source)
XLA Modules:
  0.0 505.0 jit_solution(9367897133489525281)
XLA Ops:
  6.5 1.8 copy.48
  8.4 1.5 bitcast_convert_fusion
  10.0 1.6 copy.51
  11.5 0.6 copy.52
  12.2 1.6 gather_fusion.1
  13.9 31.9 %all-gather.3.cloned.1.call-done = bf16[128,8192]{0,1:T(8,128)(2,1)} async-done(((bf16[128,1024]{0,1:T(8,128)(2,1)}), bf16[128,8192]{0,1:T(8,128)(2,1)}) %all-gather.3.cloned.1.call-update) | async-done | bytes 2097168 | tf_op jit(solution)/shard_map/all_gather | solution.py:26
  45.8 3.2 copy.49
  49.1 0.7 gather_fusion
  49.8 0.6 fusion.24
  50.5 1.2 copy.61
  51.7 139.4 %all-gather.5.cloned.1.call-done = bf16[1,64,128,128]{3,2,0,1:T(8,128)(2,1)} async-done(((bf16[1,1,128,128]{3,2,0,1:T(8,128)(2,1)}), bf16[1,64,128,128]{3,2,0,1:T(8,128)(2,1)}) %all-gather.5.cloned.1.call-update) | async-done | bytes 2097168 | tf_op jit(solution)/shard_map/all_gather | solution.py:30
  191.0 1.9 convolution_bitcast_fusion
  193.0 0.5 convolution_bitcast_fusion.1
  193.5 0.7 copy-done.1
  194.2 3.5 fusion.9
  197.7 3.8 fusion.7
  201.5 0.8 fusion.22
  202.2 0.8 fusion.20
  203.0 2.5 pad_maximum_fusion
  205.5 0.6 copy-done.4
  206.1 0.2 convert_reduce_fusion
  206.3 285.7 %all-reduce.2.cloned.1.call-done = f32[64,128,128]{2,1,0:T(8,128)} async-done(((f32[64,128,128]{2,1,0:T(8,128)}), f32[64,128,128]{2,1,0:T(8,128)}) %all-reduce.2.cloned.1.call-update) | async-done | bytes 4194320 | tf_op jit(solution)/shard_map/psum | solution.py:57
  492.0 5.8 %fusion.17 = f32[1,3,128,128]{3,1,2,0:T(4,128)S(1)} fusion(f32[64,128,128]{2,1,0:T(8,128)} %all-reduce.2.cloned.1.call-done, s32[64]{0:T(128)S(1)} %fusion.40, s32[3]{0:T(128)S(1)} %iota_add_fusion), kind=kOutput, calls=%fused_computation.24 | convolution fusion | flops 37748928 | bytes 4391180 | tf_op jit(solution)/shard_map/sk,kbc->sbc/dot_general | solution.py:60
  497.8 0.7 copy.66
  (22 shorter events, 0.2 us)
Async XLA Ops:
  6.5 39.3 %all-gather.3.cloned.1.call-start = ((), (), s32[]{:S(2)}) async-start(), calls=%async_computation | async-start | bytes 2359296 | tf_op jit(solution)/shard_map/all_gather | solution.py:26
  8.3 3.8 copy-start.3
  8.4 182.7 %all-gather.5.cloned.1.call-start = ((), (), s32[]{:S(2)}) async-start(), calls=%async_computation.1 | async-start | bytes 2129920 | tf_op jit(solution)/shard_map/all_gather | solution.py:30
  9.9 482.1 %all-reduce.2.cloned.1.call-start = ((), (), s32[]{:S(2)}) async-start(), calls=%async_computation.2 | async-start | bytes 8388608 | tf_op jit(solution)/shard_map/psum | solution.py:57
  11.5 2.3 copy-start.2
  191.0 1.9 copy-start
  192.9 1.2 copy-start.1
  205.5 0.7 copy-start.4
Sparse Core Ops, SparseCore 0:
  9.5 36.2 all-gather.2
  48.8 142.2 all-gather.4
  205.6 286.3 all-reduce.1
where the time goes:
time: 505 us
  waiting for transfers between devices  457 us (90%)
  matrix products  17 us (3%)
  between operations  13.3 us (3%)
  local copies, waits for them, and re-layouts  12.8 us (3%)
    psum x1, waiting for transfers between devices, local(): summed = lax.psum(block_grads, 'dp')  286 us
    all_gather x1, waiting for transfers between devices, local(): lax.all_gather(masters.astype(jnp.bfloat16), 'dp', axis=1, tiled=True)[0]  139 us
    all_gather x1, waiting for transfers between devices, local(): features = lax.all_gather(tokens, 'tensor', axis=1, tiled=True)  31.9 us
  transfers between devices with their start and end apart: 3, of which 3 were waited for; matrix products, arithmetic and copies ran while one was open for 2% of the time, Pallas kernels for 0%

commit v1 on v0

--- a/solution.py
+++ b/solution.py
@@ -23,7 +23,9 @@
 
 def local(tokens, hidden_grad, masters, block_row, block_col, owners):
     high = lax.Precision.HIGHEST
-    features = lax.all_gather(tokens, "tensor", axis=1, tiled=True)
+    features = jnp.concatenate(
+        lax.all_to_all(jnp.stack([tokens] * lax.axis_size("tensor")), "tensor", 0, 0), axis=1
+    )
     token_count = features.shape[0]
     block_side = masters.shape[-1]
     kept_count = block_row.shape[1]

time: 505 us -> 470 us (0.931)
  waiting for transfers between devices: 457 us -> 409 us
  starting transfers between devices: 0.09 us -> 9.47 us
    all_gather x1, waiting for transfers between devices: 139 us -> 103 us  [local(): lax.all_gather(masters.astype(jnp.bfloat16), 'dp', axis=1, tiled=True)[0]]
    all_gather x1 -> x0, waiting for transfers between devices: 31.9 us -> none  [local(): features = lax.all_gather(tokens, 'tensor', axis=1, tiled=True)]
    all_to_all x0 -> x1, waiting for transfers between devices: none -> 21.1 us  [local(): lax.all_to_all(jnp.stack([tokens] * lax.axis_size('tensor')), 'tensor', 0...]
    all_to_all x0 -> x1, starting transfers between devices: none -> 9.47 us  [local(): lax.all_to_all(jnp.stack([tokens] * lax.axis_size('tensor')), 'tensor', 0...]
  transfers between devices with their start and end apart: 3 -> 3, of which waited for: 3 -> 3; matrix products, arithmetic and copies ran while one was open for 2% -> 3% of each run, Pallas kernels for 0% -> 0%
where the time goes in v1:
time: 470 us
  waiting for transfers between devices  409 us (87%)
  matrix products  17 us (4%)
  local copies, waits for them, and re-layouts  15.6 us (3%)
  between operations  13.5 us (3%)
  starting transfers between devices  9.47 us (2%)
  other arithmetic  4.8 us (1%)
    psum x1, waiting for transfers between devices, local(): summed = lax.psum(block_grads, 'dp')  286 us
    all_gather x1, waiting for transfers between devices, local(): lax.all_gather(masters.astype(jnp.bfloat16), 'dp', axis=1, tiled=True)[0]  103 us
    all_to_all x1, waiting for transfers between devices, local(): lax.all_to_all(jnp.stack([tokens] * lax.axis_size('tensor')), 'tensor', 0...  21.1 us
    all_to_all x1, starting transfers between devices, local(): lax.all_to_all(jnp.stack([tokens] * lax.axis_size('tensor')), 'tensor', 0...  9.47 us
  transfers between devices with their start and end apart: 3, of which 3 were waited for; matrix products, arithmetic and copies ran while one was open for 3% of the time, Pallas kernels for 0%

profile of v1, /device:TPU:8, one launch (start us, length us, event | category | flops | bytes accessed | tf_op | source)
XLA Modules:
  0.0 469.8 jit_solution(12428547845631832805)
XLA Ops:
  6.5 1.5 bitcast_convert_fusion
  8.0 1.1 copy.34
  9.1 1.6 stack.2
  10.7 9.5 %all-to-all-start = ((bf16[8,128,1024]{1,2,0:T(8,128)(2,1)}), bf16[8,128,1024]{1,2,0:T(8,128)(2,1)S(1)}, u32[]{:S(2)}, u32[]{:S(2)}) async-start(bf16[8,128,1024]{1,2,0:T(8,128)(2,1)} %stack.2), calls=%async_computation | async-start | bytes 4194304 | tf_op jit(solution)/shard_map/all_to_all | solution.py:27
  20.2 1.3 copy.37
  21.5 1.6 copy.38
  23.1 1.6 gather_fusion.1
  24.8 21.1 %all-to-all-done = bf16[8,128,1024]{1,2,0:T(8,128)(2,1)S(1)} async-done(((bf16[8,128,1024]{1,2,0:T(8,128)(2,1)}), bf16[8,128,1024]{1,2,0:T(8,128)(2,1)S(1)}, u32[]{:S(2)}, u32[]{:S(2)}) %all-to-all-start) | async-done | bytes 2097184 | tf_op jit(solution)/shard_map/all_to_all | solution.py:27
  46.0 2.9 copy.35
  48.9 2.3 gather_fusion
  51.2 0.6 fusion.24
  51.9 1.2 copy.47
  53.0 102.6 %all-gather.2.cloned.1.call-done = bf16[1,64,128,128]{3,2,0,1:T(8,128)(2,1)} async-done(((bf16[1,1,128,128]{3,2,0,1:T(8,128)(2,1)}), bf16[1,64,128,128]{3,2,0,1:T(8,128)(2,1)}) %all-gather.2.cloned.1.call-update) | async-done | bytes 2097168 | tf_op jit(solution)/shard_map/all_gather | solution.py:32
  155.6 1.9 convolution_bitcast_fusion
  158.1 0.7 copy-done.1
  158.8 3.5 fusion.9
  162.3 3.8 fusion.7
  166.0 0.8 fusion.22
  166.8 0.8 fusion.20
  167.6 2.5 pad_maximum_fusion
  170.1 0.6 copy-done.5
  170.9 285.7 %all-reduce.2.cloned.1.call-done = f32[64,128,128]{2,1,0:T(8,128)} async-done(((f32[64,128,128]{2,1,0:T(8,128)}), f32[64,128,128]{2,1,0:T(8,128)}) %all-reduce.2.cloned.1.call-update) | async-done | bytes 4194320 | tf_op jit(solution)/shard_map/psum | solution.py:59
  456.5 5.8 %fusion.17 = f32[1,3,128,128]{3,1,2,0:T(4,128)S(1)} fusion(f32[64,128,128]{2,1,0:T(8,128)} %all-reduce.2.cloned.1.call-done, s32[64]{0:T(128)S(1)} %fusion.40, s32[3]{0:T(128)S(1)} %iota_add_fusion), kind=kOutput, calls=%fused_computation.24 | convolution fusion | flops 37748928 | bytes 4391180 | tf_op jit(solution)/shard_map/sk,kbc->sbc/dot_general | solution.py:62
  462.3 0.7 copy.52
  (24 shorter events, 0.8 us)
Async XLA Ops:
  6.5 149.1 %all-gather.2.cloned.1.call-start = ((), (), s32[]{:S(2)}) async-start(), calls=%async_computation.1 | async-start | bytes 2129920 | tf_op jit(solution)/shard_map/all_gather | solution.py:32
  10.7 9.5 %copy-start.2 = (bf16[128,3584]{1,0:T(8,128)(2,1)S(1)}, bf16[128,3584]{1,0:T(8,128)(2,1)}, u32[]{:S(2)}) copy-start(bf16[128,3584]{1,0:T(8,128)(2,1)} %param.7) | copy-start | bytes 2752516
  10.7 35.2 %all-to-all-start = ((bf16[8,128,1024]{1,2,0:T(8,128)(2,1)}), bf16[8,128,1024]{1,2,0:T(8,128)(2,1)S(1)}, u32[]{:S(2)}, u32[]{:S(2)}) async-start(bf16[8,128,1024]{1,2,0:T(8,128)(2,1)} %stack.2), calls=%async_computation | async-start | bytes 4194304 | tf_op jit(solution)/shard_map/all_to_all | solution.py:27
  20.2 2.9 copy-start.4
  20.2 436.3 %all-reduce.2.cloned.1.call-start = ((), (), s32[]{:S(2)}) async-start(), calls=%async_computation.2 | async-start | bytes 8388608 | tf_op jit(solution)/shard_map/psum | solution.py:59
  21.5 3.3 copy-start.3
  155.6 1.9 copy-start
  157.5 1.2 copy-start.1
  170.0 0.7 copy-start.5
Sparse Core Ops, SparseCore 0:
  10.3 145.2 all-gather.1
  170.2 286.3 all-reduce.1
